TPU v7x, 32 devices: a whole 2x2x4 slice. The times are simulated.
32 devices in a mesh: blk: 8 (over z, x), pair: 4 (over y, core).
Axes of the slice: x: 2, y: 2, z: 4, core: 2. Of those that a mesh axis runs over, the one named last changes fastest.
Arguments:
- records: bfloat16 [8, 1024, 2048], P('blk', 'pair'), may hold values from -100 to 100
- offsets: int32 [2], replicated, may hold values from 1 to 7, as said below
- source_side: int32 [8, 2], P('blk'), may hold values from 0 to 1
Outputs:
- first_side: bfloat16 [8, 2, 32, 128, 128], P('blk', None, 'pair')
- second_side: bfloat16 [8, 2, 32, 128, 128], P('blk', None, 'pair')
Inputs may be any that keep to these rules, and one draw needn't show every extreme that they name: `offsets`: distinct and increasing; the last one is 7.
All inputs are finite; a program needn't handle non-finite values.
Results may differ from a plain program's by a relative error of at most 0.012.
Values may be sent and summed in bfloat16 or wider, within the bound.
No kernel may reach another device: no remote copies, remote signals or barrier semaphores. Data moves between devices by JAX's collectives and lax.ppermute only.
A program may use at most 128 MiB of HBM per device.

v0:
```python
import math
import jax
import jax.numpy as jnp
from jax import lax
from jax.sharding import PartitionSpec as P

BLOCK_CH = 128
BINS = 128
SAMPLES = 2048
FIRST_BIN = 4
LAGS = 32


def as_sent(value):
    return jax.tree.map(lambda a: a.astype(jnp.bfloat16) if a.dtype == jnp.float32 else a, value)


def shifted_2(value, axis, steps):
    count = lax.axis_size(axis)
    leading, last = (max(0, -steps), min(count, count - steps))
    return lax.ppermute(value, axis, [(source, source + steps) for source in range(leading, last)])


def fourier_table():
    sample_index = jnp.arange(SAMPLES, dtype=jnp.int32)
    bin_index = FIRST_BIN + jnp.arange(BINS, dtype=jnp.int32)
    phase_index = sample_index[:, None] * bin_index[None, :] % SAMPLES
    angles = 2.0 * math.pi / SAMPLES * phase_index.astype(jnp.float32)
    hann_taper = 0.5 - 0.5 * jnp.cos(2.0 * math.pi / SAMPLES * sample_index.astype(jnp.float32))
    return jnp.stack(
        (hann_taper[:, None] * jnp.cos(angles), -hann_taper[:, None] * jnp.sin(angles)), axis=-1
    )


def shift_ahead(distance):
    return lambda block: jax.tree.map(
        lambda part, own: part.astype(own.dtype), shifted_2(as_sent(block), "blk", -distance), block
    )


def local(records, offsets, source_side):
    seg_local = records.shape[0]
    local_blocks = records.shape[1] // BLOCK_CH
    table_full = fourier_table()
    table_high = lax.optimization_barrier(table_full.astype(jnp.bfloat16))
    table_low = (table_full - table_high.astype(jnp.float32)).astype(jnp.bfloat16)
    traces = records.reshape(seg_local, local_blocks, BLOCK_CH, SAMPLES)
    spectrum = jnp.einsum("sbcn,nfr->bfsrc", traces, table_high, preferred_element_type=jnp.float32)
    spectrum = spectrum + jnp.einsum(
        "sbcn,nfr->bfsrc", traces, table_low, preferred_element_type=jnp.float32
    )
    band_power = jnp.sum(spectrum * spectrum, axis=3)
    band_level = jnp.mean(band_power, axis=-1)
    whiten_scale = 1.0 / jnp.sqrt(band_level + 1e-05)
    whitened = (spectrum * whiten_scale[:, :, :, None, None]).astype(jnp.bfloat16)
    regrouped = lax.all_to_all(
        lax.all_to_all(whitened, "pair", split_axis=1, concat_axis=0, tiled=True),
        "blk",
        split_axis=0,
        concat_axis=2,
        tiled=True,
    )
    own_block = regrouped[0]
    bin_local = own_block.shape[0]
    seg_total = own_block.shape[1]
    offset_total = offsets.shape[0]
    group_size = lax.axis_size("blk")
    window_size = min(16, group_size)
    bit_total = window_size.bit_length() - 1
    ahead_list = [shift_ahead(distance) for distance in range(1, window_size)]
    partners = jnp.stack(
        [lax.switch(offsets[slot] - 1, ahead_list, own_block) for slot in range(offset_total)]
    )
    reverse_side = (source_side[0] == 1)[:, None, None, None, None]
    own_many = jnp.broadcast_to(own_block[None], partners.shape)
    source = jnp.where(reverse_side, partners, own_many)
    receiver = jnp.where(reverse_side, own_many, partners)
    left_side = source.reshape(offset_total, bin_local, 2 * seg_total, BLOCK_CH)
    rotated = jnp.stack((receiver[:, :, :, 1], -receiver[:, :, :, 0]), axis=3)
    right_side = jnp.stack((receiver, rotated), axis=4).reshape(
        offset_total, bin_local, 2 * seg_total, 2, BLOCK_CH
    )
    cross = jnp.einsum(
        "kfsc,kfsrd->kfrcd", left_side, right_side, preferred_element_type=jnp.float32
    )
    cross_rows = cross.reshape(offset_total, 2 * bin_local, BLOCK_CH * BLOCK_CH)
    pair_index = lax.axis_index("pair")
    lag_index = jnp.arange(LAGS, dtype=jnp.int32) - LAGS // 2
    bin_index = FIRST_BIN + pair_index * bin_local + jnp.arange(bin_local, dtype=jnp.int32)
    phase_index = lag_index[:, None] * bin_index[None, :] % SAMPLES
    angles = 2.0 * math.pi / SAMPLES * phase_index.astype(jnp.float32)
    normalizer = 1.0 / math.sqrt(seg_total * BINS)
    lag_table = (jnp.stack((jnp.cos(angles), -jnp.sin(angles)), axis=-1) * normalizer).reshape(
        LAGS, 2 * bin_local
    )
    summed = lax.psum_scatter(
        jnp.einsum(
            "lq,kqx->lkx",
            lag_table,
            cross_rows,
            precision=lax.Precision.HIGHEST,
            preferred_element_type=jnp.float32,
        ).astype(jnp.bfloat16),
        "pair",
        scatter_dimension=0,
        tiled=True,
    ).astype(jnp.float32)
    lag_local = summed.shape[0]
    first_local = (
        summed.astype(jnp.bfloat16)
        .transpose(1, 0, 2)
        .reshape(offset_total, lag_local, BLOCK_CH, BLOCK_CH)
    )
    returned = first_local
    for bit_number in range(bit_total):
        shifted = shifted_2(returned, "blk", 1 << bit_number)
        selected = (jnp.right_shift(offsets, bit_number) % 2 == 1)[:, None, None, None]
        returned = jnp.where(selected, shifted, returned)
    return (first_local[None], returned[None])


def solution(mesh):
    placed = (P("blk", "pair", None), P(), P("blk", None))
    return jax.shard_map(
        local,
        mesh=mesh,
        in_specs=placed,
        out_specs=(P("blk", None, "pair", None, None), P("blk", None, "pair", None, None)),
        check_vma=False,
    )
```

profile of v0, /device:TPU:25, one launch (start us, length us, event | category | flops | bytes accessed | tf_op | source)
XLA Modules:
  0.0 181.7 jit_solution(7638834543979147514)
XLA Ops:
  7.2 4.2 %cosine_multiply_fusion = (f32[2048,128,1]{1,0,2:T(8,128)S(1)}, f32[2048,128,1]{1,0,2:T(8,128)S(1)}) fusion(s32[128]{0:T(128)S(1)} %iota_add_fusion, f32[2048]{0:T(1024)S(1)} %get-tuple-element.57, f32[2048]{0:T(1024)S(1)} %get-tuple-element.58), kind=kLoop, calls=%fused_computation.18 | loop fusion | flops 4194304 | bytes 2114048 | tf_op jit(solution)/shard_map/mul | solution.py:31
  13.4 4.0 %all-to-all-start = ((bf16[2,128,1,2,128]{4,0,3,2,1:T(2,128)(2,1)}), bf16[2,128,1,2,128]{4,0,3,2,1:T(2,128)(2,1)S(1)}, u32[]{:S(2)}, u32[]{:S(2)}) async-start(bf16[2,128,1,2,128]{4,0,3,2,1:T(2,128)(2,1)} %copy.65), calls=%async_computation | async-start | bytes 262144 | tf_op jit(solution)/shard_map/all_to_all | solution.py:57
  17.6 3.4 %all-to-all-done = bf16[2,128,1,2,128]{4,0,3,2,1:T(2,128)(2,1)S(1)} async-done(((bf16[2,128,1,2,128]{4,0,3,2,1:T(2,128)(2,1)}), bf16[2,128,1,2,128]{4,0,3,2,1:T(2,128)(2,1)S(1)}, u32[]{:S(2)}, u32[]{:S(2)}) %all-to-all-start) | async-done | bytes 131104 | tf_op jit(solution)/shard_map/all_to_all | solution.py:57
  21.6 5.5 %all-to-all-start.1 = ((bf16[8,32,1,2,128]{4,1,3,2,0:T(8,128)(2,1)}), bf16[8,32,1,2,128]{4,1,3,2,0:T(8,128)(2,1)S(1)}, u32[]{:S(2)}, u32[]{:S(2)}) async-start(bf16[8,32,1,2,128]{4,1,3,2,0:T(8,128)(2,1)} %bitcast.15), calls=%async_computation.1 | async-start | bytes 262144 | tf_op jit(solution)/shard_map/all_to_all | solution.py:56
  29.0 1.6 all-to-all-done.1
  30.7 4.9 %conditional.2 = (bf16[32,8,2,128]{3,2,1,0:T(2,128)(2,1)}) conditional(s32[]{:T(128)} %bitcast.19, bf16[32,8,2,128]{3,2,1,0:T(2,128)(2,1)S(1)} %copy.69, bf16[32,8,2,128]{3,2,1,0:T(2,128)(2,1)S(1)} %copy.69, bf16[32,8,2,128]{3,2,1,0:T(2,128)(2,1)S(1)} %copy.69, bf16[32,8,2,128]{3,2,1,0:T(2,128)(2,1)S(1)} %copy.69, ...), branch_computations={%region_1.2_spmd, %region_2.3_spmd, %region_3.4_spmd, %region_4.5_... | conditional | bytes 524336 | solution.py:72
  30.7 3.6 %collective-permute-start.1 = (bf16[32,8,2,128]{3,2,1,0:T(2,128)(2,1)S(1)}, bf16[32,8,2,128]{3,2,1,0:T(2,128)(2,1)}, u32[]{:S(2)}, u32[]{:S(2)}) collective-permute-start(bf16[32,8,2,128]{3,2,1,0:T(2,128)(2,1)S(1)} %param.1), channel_id=1, source_target_pairs={{8,0},{12,4},{16,8},{20,12},{24,16},{28,20},{9,1},{13,5},{17,9},{2... | collective-permute-start | bytes 393224 | tf_op jit(solution)/shard_map/cond/branch_1_fun/ppermute | solution.py:21
  34.3 1.3 collective-permute-done.1
  35.6 1.3 conditional.3
  35.6 1.3 collective-permute-start.13
  37.0 1.4 broadcast_select_fusion
  40.6 5.5 %convolution_bitcast_fusion = f32[2,32,2,128,128]{3,4,2,1,0:T(8,128)} fusion(bf16[2,32,16,1,128]{4,2,3,1,0:T(8,128)(2,1)S(1)} %bitcast.79, bf16[2,32,16,1,128]{4,2,3,1,0:T(8,128)(2,1)S(1)} %maximum_select_fusion, bf16[1,32,16,128]{3,2,1,0:T(8,128)(2,1)} %bitcast.30, bf16[1,32,16,128]{3,2,1,0:T(8,128)(2,1)} %bitcast.29, ...), kind=kOutput, calls=%fused_computation.2 | convolution fusion | flops 67633152 | bytes 9306114 | tf_op jit(solution)/shard_map/kfsc,kfsrd->kfrcd/dot_general | solution.py:83
  46.1 8.9 %copy.85 = f32[2,32,2,128,128]{4,3,2,1,0:T(8,128)} copy(f32[2,32,2,128,128]{3,4,2,1,0:T(8,128)} %convolution_bitcast_fusion) | data formatting | bytes 16777216 | tf_op jit(solution)/shard_map/kfsc,kfsrd->kfrcd/transpose | solution.py:83
  55.0 9.4 %reshape.414 = f32[2,64,16384]{2,1,0:T(8,128)} reshape(f32[2,32,2,128,128]{4,3,2,1,0:T(8,128)} %copy.85) | data formatting | bytes 16777216 | tf_op jit(solution)/shard_map/reshape | solution.py:86
  64.4 6.4 %fusion = bf16[2,4,8,16384]{3,2,1,0:T(8,128)(2,1)S(1)} fusion(f32[32,64,1]{0,1,2:T(8,128)S(1)} %bitcast.81, f32[2,64,16384]{2,1,0:T(8,128)} %reshape.414), kind=kOutput, calls=%fused_computation.1 | convolution fusion | flops 806354944 | bytes 10493952 | tf_op jit(solution)/shard_map/lq,kqx->lkx/dot_general | solution.py:97
  70.9 1.5 copy.97
  72.4 42.0 %reduce-scatter.4.cloned.1.call-done = bf16[8,32768]{1,0:T(8,128)(2,1)} async-done(((bf16[32,32768]{1,0:T(8,128)(2,1)}), bf16[8,32768]{1,0:T(8,128)(2,1)}) %reduce-scatter.4.cloned.1.call-update) | async-done | bytes 524304
  114.4 1.2 copy.87
  115.6 3.1 %collective-permute-start.14 = (bf16[2,8,128,128]{3,2,1,0:T(8,128)(2,1)S(1)}, bf16[2,8,128,128]{3,2,1,0:T(8,128)(2,1)S(1)}, u32[]{:S(2)}, u32[]{:S(2)}) collective-permute-start(bf16[2,8,128,128]{3,2,1,0:T(8,128)(2,1)S(1)} %copy.87), channel_id=1, source_target_pairs={{0,4},{4,8},{8,12},{12,16},{16,20},{20,24},{24,28},{1,5},{5,9},{9,... | collective-permute-start | bytes 1572872 | tf_op jit(solution)/shard_map/ppermute | solution.py:21
  118.8 12.3 %collective-permute-done.14 = bf16[2,8,128,128]{3,2,1,0:T(8,128)(2,1)S(1)} collective-permute-done((bf16[2,8,128,128]{3,2,1,0:T(8,128)(2,1)S(1)}, bf16[2,8,128,128]{3,2,1,0:T(8,128)(2,1)S(1)}, u32[]{:S(2)}, u32[]{:S(2)}) %collective-permute-start.14) | collective-permute-done | bytes 524320 | tf_op jit(solution)/shard_map/ppermute | solution.py:21
  132.2 1.3 collective-permute-start.15
  133.5 12.4 %collective-permute-done.15 = bf16[2,8,128,128]{3,2,1,0:T(8,128)(2,1)S(1)} collective-permute-done((bf16[2,8,128,128]{3,2,1,0:T(8,128)(2,1)S(1)}, bf16[2,8,128,128]{3,2,1,0:T(8,128)(2,1)S(1)}, u32[]{:S(2)}, u32[]{:S(2)}) %collective-permute-start.15) | collective-permute-done | bytes 524320 | tf_op jit(solution)/shard_map/ppermute | solution.py:21
  146.0 1.3 collective-permute-start.16
  148.2 25.7 %collective-permute-done.16 = bf16[2,8,128,128]{3,2,1,0:T(8,128)(2,1)S(1)} collective-permute-done((bf16[2,8,128,128]{3,2,1,0:T(8,128)(2,1)S(1)}, bf16[2,8,128,128]{3,2,1,0:T(8,128)(2,1)S(1)}, u32[]{:S(2)}, u32[]{:S(2)}) %collective-permute-start.16) | collective-permute-done | bytes 524320 | tf_op jit(solution)/shard_map/ppermute | solution.py:21
  (37 shorter events, 8.9 us)
Async XLA Ops:
  7.2 4.4 %copy-start = (bf16[1,256,2048]{2,1,0:T(8,128)(2,1)S(1)}, bf16[1,256,2048]{2,1,0:T(8,128)(2,1)}, u32[]{:S(2)}) copy-start(bf16[1,256,2048]{2,1,0:T(8,128)(2,1)} %param.17) | copy-start | bytes 3145732
  11.6 15.5 %copy-start.2 = (s32[2]{0:T(128)S(1)}, s32[2]{0:T(128)}, u32[]{:S(2)}) copy-start(s32[2]{0:T(128)} %param.18) | copy-start | bytes 28
  11.6 17.4 %copy-start.3 = (s32[1,2]{1,0:T(1,128)S(1)}, s32[1,2]{1,0:T(1,128)}, u32[]{:S(2)}) copy-start(s32[1,2]{1,0:T(1,128)} %param.19) | copy-start | bytes 28
  13.4 7.5 %all-to-all-start = ((bf16[2,128,1,2,128]{4,0,3,2,1:T(2,128)(2,1)}), bf16[2,128,1,2,128]{4,0,3,2,1:T(2,128)(2,1)S(1)}, u32[]{:S(2)}, u32[]{:S(2)}) async-start(bf16[2,128,1,2,128]{4,0,3,2,1:T(2,128)(2,1)} %copy.65), calls=%async_computation | async-start | bytes 262144 | tf_op jit(solution)/shard_map/all_to_all | solution.py:57
  21.6 8.9 %all-to-all-start.1 = ((bf16[8,32,1,2,128]{4,1,3,2,0:T(8,128)(2,1)}), bf16[8,32,1,2,128]{4,1,3,2,0:T(8,128)(2,1)S(1)}, u32[]{:S(2)}, u32[]{:S(2)}) async-start(bf16[8,32,1,2,128]{4,1,3,2,0:T(8,128)(2,1)} %bitcast.15), calls=%async_computation.1 | async-start | bytes 262144 | tf_op jit(solution)/shard_map/all_to_all | solution.py:56
  27.1 87.3 %reduce-scatter.4.cloned.1.call-start = ((), (), s32[]{:S(2)}) async-start(), calls=%async_computation.3 | async-start | bytes 2621440
  30.7 4.9 %collective-permute-start.1 = (bf16[32,8,2,128]{3,2,1,0:T(2,128)(2,1)S(1)}, bf16[32,8,2,128]{3,2,1,0:T(2,128)(2,1)}, u32[]{:S(2)}, u32[]{:S(2)}) collective-permute-start(bf16[32,8,2,128]{3,2,1,0:T(2,128)(2,1)S(1)} %param.1), channel_id=1, source_target_pairs={{8,0},{12,4},{16,8},{20,12},{24,16},{28,20},{9,1},{13,5},{17,9},{2... | collective-permute-start | bytes 393224 | tf_op jit(solution)/shard_map/cond/branch_1_fun/ppermute | solution.py:21
  35.6 1.3 collective-permute-start.13
  114.4 32.9 %copy-start.1 = (bf16[8,32768]{1,0:T(8,128)(2,1)S(1)}, bf16[8,32768]{1,0:T(8,128)(2,1)}, u32[]{:S(2)}) copy-start(bf16[8,32768]{1,0:T(8,128)(2,1)} %reduce-scatter.4.cloned.1.call-done) | copy-start | bytes 1572868
  115.6 15.4 %collective-permute-start.14 = (bf16[2,8,128,128]{3,2,1,0:T(8,128)(2,1)S(1)}, bf16[2,8,128,128]{3,2,1,0:T(8,128)(2,1)S(1)}, u32[]{:S(2)}, u32[]{:S(2)}) collective-permute-start(bf16[2,8,128,128]{3,2,1,0:T(8,128)(2,1)S(1)} %copy.87), channel_id=1, source_target_pairs={{0,4},{4,8},{8,12},{12,16},{16,20},{20,24},{24,28},{1,5},{5,9},{9,... | collective-permute-start | bytes 1572872 | tf_op jit(solution)/shard_map/ppermute | solution.py:21
  132.2 13.7 %collective-permute-start.15 = (bf16[2,8,128,128]{3,2,1,0:T(8,128)(2,1)S(1)}, bf16[2,8,128,128]{3,2,1,0:T(8,128)(2,1)S(1)}, u32[]{:S(2)}, u32[]{:S(2)}) collective-permute-start(bf16[2,8,128,128]{3,2,1,0:T(8,128)(2,1)S(1)} %broadcast_select_fusion.1), channel_id=1, source_target_pairs={{0,8},{4,12},{8,16},{12,20},{16,24},{20,28},{1,9},{5,13},{9,17},{1... | collective-permute-start | bytes 1572872 | tf_op jit(solution)/shard_map/ppermute | solution.py:21
  146.0 27.9 %collective-permute-start.16 = (bf16[2,8,128,128]{3,2,1,0:T(8,128)(2,1)S(1)}, bf16[2,8,128,128]{3,2,1,0:T(8,128)(2,1)S(1)}, u32[]{:S(2)}, u32[]{:S(2)}) collective-permute-start(bf16[2,8,128,128]{3,2,1,0:T(8,128)(2,1)S(1)} %broadcast_select_fusion.2), channel_id=1, source_target_pairs={{0,16},{4,20},{8,24},{12,28},{1,17},{5,21},{9,25},{13,29},{2,18},{... | collective-permute-start | bytes 1572872 | tf_op jit(solution)/shard_map/ppermute | solution.py:21
Sparse Core Ops, SparseCore 0:
  72.5 41.8 reduce-scatter.3
where the time goes:
time: 183 us; the launch traced here: 182 us
  waiting for transfers between devices  98.6 us (54%)
  local copies, waits for them, and re-layouts  24.2 us (13%)
  starting transfers between devices  20 us (11%)
  between operations  15.4 us (8%)
  matrix products  12.9 us (7%)
  other arithmetic  10.4 us (6%)
    ppermute x5, waiting for transfers between devices, shifted_2(): lax.ppermute(value, axis, [(source, source + steps) for source in range(l...  51.6 us
    unnamed x2, waiting for transfers between devices  42 us
    ppermute x5, starting transfers between devices, shifted_2(): lax.ppermute(value, axis, [(source, source + steps) for source in range(l...  10.6 us
    reshape x1, local copies, waits for them, and re-layouts, local(): cross_rows = cross.reshape(offset_total, 2 * bin_local, BLOCK_CH * BLOCK_CH)  9.44 us
    transpose x1, local copies, waits for them, and re-layouts, local(): jnp.einsum('kfsc,kfsrd->kfrcd', left_side, right_side, preferred_element_...  8.89 us
    dot_general x1, matrix products, local(): jnp.einsum('lq,kqx->lkx', lag_table, cross_rows, precision=lax.Precision....  6.43 us
    dot_general x1, matrix products, local(): jnp.einsum('kfsc,kfsrd->kfrcd', left_side, right_side, preferred_element_...  5.54 us
    all_to_all x1, starting transfers between devices, local(): lax.all_to_all(lax.all_to_all(whitened, 'pair', split_axis=1, concat_axis...  5.46 us
  transfers between devices with their start and end apart: 8, of which 7 were waited for; matrix products, arithmetic and copies ran while one was open for 1% of the time, Pallas kernels for 0%

commit v1 on v0

--- a/solution.py
+++ b/solution.py
@@ -53,12 +53,20 @@
     band_level = jnp.mean(band_power, axis=-1)
     whiten_scale = 1.0 / jnp.sqrt(band_level + 1e-05)
     whitened = (spectrum * whiten_scale[:, :, :, None, None]).astype(jnp.bfloat16)
-    regrouped = lax.all_to_all(
-        lax.all_to_all(whitened, "pair", split_axis=1, concat_axis=0, tiled=True),
-        "blk",
-        split_axis=0,
-        concat_axis=2,
-        tiled=True,
+    regrouped = jnp.concatenate(
+        lax.all_to_all(
+            jnp.stack(
+                jnp.split(
+                    lax.all_to_all(whitened, "pair", split_axis=1, concat_axis=0, tiled=True),
+                    lax.axis_size("blk"),
+                    axis=0,
+                )
+            ),
+            "blk",
+            0,
+            0,
+        ),
+        axis=2,
     )
     own_block = regrouped[0]
     bin_local = own_block.shape[0]

time: 183 us -> 187 us (1.022)
  local copies, waits for them, and re-layouts: 24.2 us -> 28.4 us
    unnamed x10 -> x17, local copies, waits for them, and re-layouts: 2.42 us -> 6.67 us
where the time goes in v1:
time: 187 us; the launch traced here: 186 us
  waiting for transfers between devices  98.6 us (53%)
  local copies, waits for them, and re-layouts  28.4 us (15%)
  starting transfers between devices  20 us (11%)
  between operations  15.4 us (8%)
  matrix products  12.9 us (7%)
  other arithmetic  10.4 us (6%)
    ppermute x5, waiting for transfers between devices, shifted_2(): lax.ppermute(value, axis, [(source, source + steps) for source in range(l...  51.6 us
    unnamed x2, waiting for transfers between devices  42 us
    ppermute x5, starting transfers between devices, shifted_2(): lax.ppermute(value, axis, [(source, source + steps) for source in range(l...  10.6 us
    reshape x1, local copies, waits for them, and re-layouts, local(): cross_rows = cross.reshape(offset_total, 2 * bin_local, BLOCK_CH * BLOCK_CH)  9.44 us
    transpose x1, local copies, waits for them, and re-layouts, local(): jnp.einsum('kfsc,kfsrd->kfrcd', left_side, right_side, preferred_element_...  8.89 us
    unnamed x17, local copies, waits for them, and re-layouts  6.67 us
    dot_general x1, matrix products, local(): jnp.einsum('lq,kqx->lkx', lag_table, cross_rows, precision=lax.Precision....  6.43 us
    dot_general x1, matrix products, local(): jnp.einsum('kfsc,kfsrd->kfrcd', left_side, right_side, preferred_element_...  5.54 us
  transfers between devices with their start and end apart: 8, of which 7 were waited for; matrix products, arithmetic and copies ran while one was open for 1% of the time, Pallas kernels for 0%

profile of v1, /device:TPU:25, one launch (start us, length us, event | category | flops | bytes accessed | tf_op | source)
XLA Modules:
  0.0 185.8 jit_solution(17263714962167585406)
XLA Ops:
  7.2 4.2 %cosine_multiply_fusion = (f32[2048,128,1]{1,0,2:T(8,128)S(1)}, f32[2048,128,1]{1,0,2:T(8,128)S(1)}) fusion(s32[128]{0:T(128)S(1)} %iota_add_fusion, f32[2048]{0:T(1024)S(1)} %get-tuple-element.57, f32[2048]{0:T(1024)S(1)} %get-tuple-element.58), kind=kLoop, calls=%fused_computation.18 | loop fusion | flops 4194304 | bytes 2114048 | tf_op jit(solution)/shard_map/mul | solution.py:31
  13.4 4.0 %all-to-all-start = ((bf16[2,128,1,2,128]{4,0,3,2,1:T(2,128)(2,1)}), bf16[2,128,1,2,128]{4,0,3,2,1:T(2,128)(2,1)S(1)}, u32[]{:S(2)}, u32[]{:S(2)}) async-start(bf16[2,128,1,2,128]{4,0,3,2,1:T(2,128)(2,1)} %copy.79), calls=%async_computation | async-start | bytes 262144 | tf_op jit(solution)/shard_map/all_to_all | solution.py:60
  17.6 3.4 %all-to-all-done = bf16[2,128,1,2,128]{4,0,3,2,1:T(2,128)(2,1)S(1)} async-done(((bf16[2,128,1,2,128]{4,0,3,2,1:T(2,128)(2,1)}), bf16[2,128,1,2,128]{4,0,3,2,1:T(2,128)(2,1)S(1)}, u32[]{:S(2)}, u32[]{:S(2)}) %all-to-all-start) | async-done | bytes 131104 | tf_op jit(solution)/shard_map/all_to_all | solution.py:60
  25.8 5.5 %all-to-all-start.1 = ((bf16[8,1,32,1,2,128]{5,2,4,3,1,0:T(8,128)(2,1)}), bf16[8,1,32,1,2,128]{5,2,4,3,1,0:T(8,128)(2,1)S(1)}, u32[]{:S(2)}, u32[]{:S(2)}) async-start(bf16[8,1,32,1,2,128]{5,2,4,3,1,0:T(8,128)(2,1)} %constant_dynamic-update-slice_fusion), calls=%async_computation.1 | async-start | bytes 262144 | tf_op jit(solution)/shard_map/all_to_all | solution.py:57
  33.2 1.6 all-to-all-done.1
  34.9 4.9 %conditional.2 = (bf16[32,8,2,128]{3,2,1,0:T(2,128)(2,1)}) conditional(s32[]{:T(128)} %bitcast.26, bf16[32,8,2,128]{3,2,1,0:T(2,128)(2,1)S(1)} %copy.83, bf16[32,8,2,128]{3,2,1,0:T(2,128)(2,1)S(1)} %copy.83, bf16[32,8,2,128]{3,2,1,0:T(2,128)(2,1)S(1)} %copy.83, bf16[32,8,2,128]{3,2,1,0:T(2,128)(2,1)S(1)} %copy.83, ...), branch_computations={%region_1.2_spmd, %region_2.3_spmd, %region_3.4_spmd, %region_4.5_... | conditional | bytes 524336 | solution.py:80
  34.9 3.6 %collective-permute-start.1 = (bf16[32,8,2,128]{3,2,1,0:T(2,128)(2,1)S(1)}, bf16[32,8,2,128]{3,2,1,0:T(2,128)(2,1)}, u32[]{:S(2)}, u32[]{:S(2)}) collective-permute-start(bf16[32,8,2,128]{3,2,1,0:T(2,128)(2,1)S(1)} %param.1), channel_id=1, source_target_pairs={{8,0},{12,4},{16,8},{20,12},{24,16},{28,20},{9,1},{13,5},{17,9},{2... | collective-permute-start | bytes 393224 | tf_op jit(solution)/shard_map/cond/branch_1_fun/ppermute | solution.py:21
  38.5 1.3 collective-permute-done.1
  39.8 1.3 conditional.3
  39.8 1.3 collective-permute-start.13
  41.2 1.4 broadcast_select_fusion
  44.8 5.5 %convolution_bitcast_fusion = f32[2,32,2,128,128]{3,4,2,1,0:T(8,128)} fusion(bf16[2,32,16,1,128]{4,2,3,1,0:T(8,128)(2,1)S(1)} %bitcast.109, bf16[2,32,16,1,128]{4,2,3,1,0:T(8,128)(2,1)S(1)} %maximum_select_fusion, bf16[1,32,16,128]{3,2,1,0:T(8,128)(2,1)} %bitcast.36, bf16[1,32,16,128]{3,2,1,0:T(8,128)(2,1)} %bitcast.35, ...), kind=kOutput, calls=%fused_computation.2 | convolution fusion | flops 67633152 | bytes 9306114 | tf_op jit(solution)/shard_map/kfsc,kfsrd->kfrcd/dot_general | solution.py:91
  50.3 8.9 %copy.99 = f32[2,32,2,128,128]{4,3,2,1,0:T(8,128)} copy(f32[2,32,2,128,128]{3,4,2,1,0:T(8,128)} %convolution_bitcast_fusion) | data formatting | bytes 16777216 | tf_op jit(solution)/shard_map/kfsc,kfsrd->kfrcd/transpose | solution.py:91
  59.2 9.4 %reshape.417 = f32[2,64,16384]{2,1,0:T(8,128)} reshape(f32[2,32,2,128,128]{4,3,2,1,0:T(8,128)} %copy.99) | data formatting | bytes 16777216 | tf_op jit(solution)/shard_map/reshape | solution.py:94
  68.6 6.4 %fusion = bf16[2,4,8,16384]{3,2,1,0:T(8,128)(2,1)S(1)} fusion(f32[32,64,1]{0,1,2:T(8,128)S(1)} %bitcast.119, f32[2,64,16384]{2,1,0:T(8,128)} %reshape.417), kind=kOutput, calls=%fused_computation.1 | convolution fusion | flops 806354944 | bytes 10493952 | tf_op jit(solution)/shard_map/lq,kqx->lkx/dot_general | solution.py:105
  75.1 1.5 copy.111
  76.6 42.0 %reduce-scatter.4.cloned.1.call-done = bf16[8,32768]{1,0:T(8,128)(2,1)} async-done(((bf16[32,32768]{1,0:T(8,128)(2,1)}), bf16[8,32768]{1,0:T(8,128)(2,1)}) %reduce-scatter.4.cloned.1.call-update) | async-done | bytes 524304
  118.6 1.2 copy.101
  119.8 3.1 %collective-permute-start.14 = (bf16[2,8,128,128]{3,2,1,0:T(8,128)(2,1)S(1)}, bf16[2,8,128,128]{3,2,1,0:T(8,128)(2,1)S(1)}, u32[]{:S(2)}, u32[]{:S(2)}) collective-permute-start(bf16[2,8,128,128]{3,2,1,0:T(8,128)(2,1)S(1)} %copy.101), channel_id=1, source_target_pairs={{0,4},{4,8},{8,12},{12,16},{16,20},{20,24},{24,28},{1,5},{5,9},{9,... | collective-permute-start | bytes 1572872 | tf_op jit(solution)/shard_map/ppermute | solution.py:21
  123.0 12.3 %collective-permute-done.14 = bf16[2,8,128,128]{3,2,1,0:T(8,128)(2,1)S(1)} collective-permute-done((bf16[2,8,128,128]{3,2,1,0:T(8,128)(2,1)S(1)}, bf16[2,8,128,128]{3,2,1,0:T(8,128)(2,1)S(1)}, u32[]{:S(2)}, u32[]{:S(2)}) %collective-permute-start.14) | collective-permute-done | bytes 524320 | tf_op jit(solution)/shard_map/ppermute | solution.py:21
  136.4 1.3 collective-permute-start.15
  137.7 12.4 %collective-permute-done.15 = bf16[2,8,128,128]{3,2,1,0:T(8,128)(2,1)S(1)} collective-permute-done((bf16[2,8,128,128]{3,2,1,0:T(8,128)(2,1)S(1)}, bf16[2,8,128,128]{3,2,1,0:T(8,128)(2,1)S(1)}, u32[]{:S(2)}, u32[]{:S(2)}) %collective-permute-start.15) | collective-permute-done | bytes 524320 | tf_op jit(solution)/shard_map/ppermute | solution.py:21
  150.2 1.3 collective-permute-start.16
  152.4 25.6 %collective-permute-done.16 = bf16[2,8,128,128]{3,2,1,0:T(8,128)(2,1)S(1)} collective-permute-done((bf16[2,8,128,128]{3,2,1,0:T(8,128)(2,1)S(1)}, bf16[2,8,128,128]{3,2,1,0:T(8,128)(2,1)S(1)}, u32[]{:S(2)}, u32[]{:S(2)}) %collective-permute-start.16) | collective-permute-done | bytes 524320 | tf_op jit(solution)/shard_map/ppermute | solution.py:21
  (45 shorter events, 13.1 us)
Async XLA Ops:
  7.2 4.4 %copy-start = (bf16[1,256,2048]{2,1,0:T(8,128)(2,1)S(1)}, bf16[1,256,2048]{2,1,0:T(8,128)(2,1)}, u32[]{:S(2)}) copy-start(bf16[1,256,2048]{2,1,0:T(8,128)(2,1)} %param.17) | copy-start | bytes 3145732
  11.6 19.7 %copy-start.2 = (s32[2]{0:T(128)S(1)}, s32[2]{0:T(128)}, u32[]{:S(2)}) copy-start(s32[2]{0:T(128)} %param.18) | copy-start | bytes 28
  11.6 21.6 %copy-start.3 = (s32[1,2]{1,0:T(1,128)S(1)}, s32[1,2]{1,0:T(1,128)}, u32[]{:S(2)}) copy-start(s32[1,2]{1,0:T(1,128)} %param.19) | copy-start | bytes 28
  13.4 7.5 %all-to-all-start = ((bf16[2,128,1,2,128]{4,0,3,2,1:T(2,128)(2,1)}), bf16[2,128,1,2,128]{4,0,3,2,1:T(2,128)(2,1)S(1)}, u32[]{:S(2)}, u32[]{:S(2)}) async-start(bf16[2,128,1,2,128]{4,0,3,2,1:T(2,128)(2,1)} %copy.79), calls=%async_computation | async-start | bytes 262144 | tf_op jit(solution)/shard_map/all_to_all | solution.py:60
  25.8 8.9 %all-to-all-start.1 = ((bf16[8,1,32,1,2,128]{5,2,4,3,1,0:T(8,128)(2,1)}), bf16[8,1,32,1,2,128]{5,2,4,3,1,0:T(8,128)(2,1)S(1)}, u32[]{:S(2)}, u32[]{:S(2)}) async-start(bf16[8,1,32,1,2,128]{5,2,4,3,1,0:T(8,128)(2,1)} %constant_dynamic-update-slice_fusion), calls=%async_computation.1 | async-start | bytes 262144 | tf_op jit(solution)/shard_map/all_to_all | solution.py:57
  31.3 87.3 %reduce-scatter.4.cloned.1.call-start = ((), (), s32[]{:S(2)}) async-start(), calls=%async_computation.3 | async-start | bytes 2621440
  34.9 4.9 %collective-permute-start.1 = (bf16[32,8,2,128]{3,2,1,0:T(2,128)(2,1)S(1)}, bf16[32,8,2,128]{3,2,1,0:T(2,128)(2,1)}, u32[]{:S(2)}, u32[]{:S(2)}) collective-permute-start(bf16[32,8,2,128]{3,2,1,0:T(2,128)(2,1)S(1)} %param.1), channel_id=1, source_target_pairs={{8,0},{12,4},{16,8},{20,12},{24,16},{28,20},{9,1},{13,5},{17,9},{2... | collective-permute-start | bytes 393224 | tf_op jit(solution)/shard_map/cond/branch_1_fun/ppermute | solution.py:21
  39.8 1.3 collective-permute-start.13
  118.6 32.9 %copy-start.1 = (bf16[8,32768]{1,0:T(8,128)(2,1)S(1)}, bf16[8,32768]{1,0:T(8,128)(2,1)}, u32[]{:S(2)}) copy-start(bf16[8,32768]{1,0:T(8,128)(2,1)} %reduce-scatter.4.cloned.1.call-done) | copy-start | bytes 1572868
  119.8 15.4 %collective-permute-start.14 = (bf16[2,8,128,128]{3,2,1,0:T(8,128)(2,1)S(1)}, bf16[2,8,128,128]{3,2,1,0:T(8,128)(2,1)S(1)}, u32[]{:S(2)}, u32[]{:S(2)}) collective-permute-start(bf16[2,8,128,128]{3,2,1,0:T(8,128)(2,1)S(1)} %copy.101), channel_id=1, source_target_pairs={{0,4},{4,8},{8,12},{12,16},{16,20},{20,24},{24,28},{1,5},{5,9},{9,... | collective-permute-start | bytes 1572872 | tf_op jit(solution)/shard_map/ppermute | solution.py:21
  136.4 13.7 %collective-permute-start.15 = (bf16[2,8,128,128]{3,2,1,0:T(8,128)(2,1)S(1)}, bf16[2,8,128,128]{3,2,1,0:T(8,128)(2,1)S(1)}, u32[]{:S(2)}, u32[]{:S(2)}) collective-permute-start(bf16[2,8,128,128]{3,2,1,0:T(8,128)(2,1)S(1)} %broadcast_select_fusion.1), channel_id=1, source_target_pairs={{0,8},{4,12},{8,16},{12,20},{16,24},{20,28},{1,9},{5,13},{9,17},{1... | collective-permute-start | bytes 1572872 | tf_op jit(solution)/shard_map/ppermute | solution.py:21
  150.2 27.8 %collective-permute-start.16 = (bf16[2,8,128,128]{3,2,1,0:T(8,128)(2,1)S(1)}, bf16[2,8,128,128]{3,2,1,0:T(8,128)(2,1)S(1)}, u32[]{:S(2)}, u32[]{:S(2)}) collective-permute-start(bf16[2,8,128,128]{3,2,1,0:T(8,128)(2,1)S(1)} %broadcast_select_fusion.2), channel_id=1, source_target_pairs={{0,16},{4,20},{8,24},{12,28},{1,17},{5,21},{9,25},{13,29},{2,18},{... | collective-permute-start | bytes 1572872 | tf_op jit(solution)/shard_map/ppermute | solution.py:21
Sparse Core Ops, SparseCore 0:
  76.7 41.8 reduce-scatter.3
